TPU v7x, 32 devices: a whole 2x2x4 slice. The times are simulated.
32 devices in a mesh: seq: 4 (over x, core), grp: 8 (over z, y).
Axes of the slice: x: 2, y: 2, z: 4, core: 2. Of those that a mesh axis runs over, the one named last changes fastest.
Arguments:
- conv_input: bfloat16 [8, 512, 2688], P('grp', 'seq'), may hold values from -6 to 6
- conv_weight: float32 [4, 2688], replicated, may hold values from -3 to 3
- step_raw: float32 [8, 512, 40], P('grp', 'seq'), may hold values from -9 to 6
- rate_log: float32 [40], replicated, may hold values from -3 to 3.1
- skip_gain: float32 [40], replicated, may hold values from 0.5 to 1.5
- gate_input: bfloat16 [8, 512, 2560], P('grp', 'seq'), may hold values from -6 to 6
- norm_gain: float32 [2560], replicated, may hold values from 0.1 to 1.9
- out_weight: bfloat16 [2560, 2560], P('grp'), may hold values from -0.125 to 0.125
- residual: bfloat16 [8, 512, 2560], P('grp', 'seq'), may hold values from -6 to 6
- moe_gain: float32 [2560], replicated, may hold values from 0.1 to 1.9
- w_gate: bfloat16 [8, 2560, 512], P('grp'), may hold values from -0.125 to 0.125
- w_up: bfloat16 [8, 2560, 512], P('grp'), may hold values from -0.125 to 0.125
- w_down: bfloat16 [8, 512, 2560], P('grp'), may hold values from -0.25 to 0.25
- routes: int32 [8, 512, 2], P('grp', 'seq'), may hold values from 0 to 7, as said below
- route_weights: float32 [8, 512, 2], P('grp', 'seq'), may hold values from 0.2 to 1
Outputs:
- layer_out: bfloat16 [8, 512, 2560], P('grp', 'seq')
Inputs may be any that keep to these rules, and one draw needn't show every extreme that they name: `routes`: within the rows of one device (each aligned block of 128 frames of one manuscript) no expert is named by more than 64 entries, and one expert, the same in every block, is named by exactly 64; the two entries of a frame differ.
All inputs are finite; a program needn't handle non-finite values.
Results may differ from a plain program's by a relative error of at most 0.012.
Values may be sent and summed in bfloat16 or wider, within the bound.
A program may use at most 128 MiB of HBM per device.

v0:
```python
import jax
import jax.numpy as jnp
from jax import lax
from jax.sharding import PartitionSpec as P

EPSILON = 1e-05


def from_behind(value, axis, steps):
    count = lax.axis_size(axis)
    first, last = (max(0, -steps), min(count, count - steps))
    return lax.ppermute(value, axis, [(source, source + steps) for source in range(first, last)])


def on_device(
    conv_input,
    conv_weight,
    step_raw,
    rate_log,
    skip_gain,
    gate_input,
    norm_gain,
    out_weight,
    residual,
    moe_gain,
    w_gate,
    w_up,
    w_down,
    routes,
    route_weights,
):
    half = jnp.bfloat16
    ring = lax.axis_size("seq")
    own = lax.axis_index("seq")
    share = out_weight.shape[1] // ring
    weight_share = lax.all_gather(
        lax.dynamic_slice_in_dim(out_weight, own * share, share, axis=1), "grp", axis=0, tiled=True
    )
    frames_in = conv_input[0]
    row_count = frames_in.shape[0]
    tap_count = conv_weight.shape[0]
    channel_count = conv_weight.shape[1]
    head_count = rate_log.shape[0]
    inner_width = gate_input.shape[2]
    head_width = inner_width // head_count
    state_width = (channel_count - inner_width) // 2
    model_width = residual.shape[2]
    edge_rows = frames_in[row_count - (tap_count - 1) :]
    before = from_behind(edge_rows, "seq", 1)
    padded = jnp.concatenate([before, frames_in], axis=0).astype(jnp.float32)
    summed = conv_weight[0][None, :] * padded[0:row_count]
    for offset in range(1, tap_count):
        summed = summed + conv_weight[offset][None, :] * padded[offset : offset + row_count]
    signal = jax.nn.silu(summed).astype(jnp.bfloat16)
    x_part = signal[:, :inner_width]
    b_part = signal[:, inner_width : inner_width + state_width]
    c_part = signal[:, inner_width + state_width :]
    step_size = jax.nn.softplus(step_raw[0])
    log_decay = -step_size * jnp.exp(rate_log)[None, :]
    cumulative = jnp.cumsum(log_decay, axis=0)
    x_values = x_part.astype(jnp.float32).reshape(row_count, head_count, head_width)
    b_values = b_part.astype(jnp.float32)
    c_values = c_part.astype(jnp.float32)
    scores = jnp.dot(c_part, b_part.T, preferred_element_type=jnp.float32)
    positions = jnp.arange(row_count)
    causal = positions[:, None] >= positions[None, :]
    by_head = cumulative.T
    gap_log = by_head[:, :, None] - by_head[:, None, :]
    decay_mask = jnp.where(causal[None], jnp.exp(jnp.where(causal[None], gap_log, 0.0)), 0.0)
    mixing = (scores[None] * decay_mask * step_size.T[:, None, :]).astype(half)
    x_heads = x_part.reshape(row_count, head_count, head_width)
    tail_weight = jnp.exp(cumulative[-1][None, :] - cumulative) * step_size
    local_state = jnp.einsum(
        "shp,sn->hpn",
        (x_values * tail_weight[:, :, None]).astype(half),
        b_part,
        preferred_element_type=jnp.float32,
    ).astype(half)
    totals = lax.all_gather(cumulative[-1], "seq", axis=0)
    passing = jnp.zeros_like(totals[0])
    entering = jnp.zeros(local_state.shape, jnp.float32)
    for shift in range(1, ring):
        arrived_state = from_behind(local_state, "seq", shift).astype(jnp.float32)
        entering = entering + jnp.exp(passing)[:, None, None] * arrived_state
        passing = passing + totals[jnp.maximum(own - shift, 0)]
    within = jnp.einsum("hts,shp->thp", mixing, x_heads, preferred_element_type=jnp.float32)
    carried = (
        jnp.einsum("tn,hpn->thp", c_part, entering.astype(half), preferred_element_type=jnp.float32)
        * jnp.exp(cumulative)[:, :, None]
    )
    ssd_out = (within + carried + skip_gain[None, :, None] * x_values).reshape(
        row_count, inner_width
    )
    gated_out = ssd_out * jax.nn.silu(gate_input[0].astype(jnp.float32))
    mean_square = jnp.mean(gated_out * gated_out, axis=1, keepdims=True)
    normed = (gated_out * lax.rsqrt(mean_square + EPSILON) * norm_gain[None, :]).astype(
        jnp.bfloat16
    )
    all_rows = lax.all_gather(normed, "seq", axis=0, tiled=True)
    column_share = jnp.dot(all_rows, weight_share, preferred_element_type=jnp.float32).astype(half)
    projected = lax.all_to_all(column_share, "seq", split_axis=0, concat_axis=1, tiled=True).astype(
        jnp.float32
    )
    mixed_out = (residual[0].astype(jnp.float32) + projected).astype(jnp.bfloat16)
    mixed_float = mixed_out.astype(jnp.float32)
    mixed_square = jnp.mean(mixed_float * mixed_float, axis=1, keepdims=True)
    moe_in = (mixed_float * lax.rsqrt(mixed_square + EPSILON) * moe_gain[None, :]).astype(
        jnp.bfloat16
    )
    experts = lax.axis_size("grp")
    capacity = 4 * row_count // experts
    flat_picks = routes[0].reshape(-1)
    member = (flat_picks[:, None] == jnp.arange(experts)[None, :]).astype(jnp.int32)
    position = jnp.cumsum(member, axis=0) - member
    slot_index = jnp.sum(position * member, axis=1)
    target = (flat_picks * capacity + slot_index).reshape(row_count, 2)
    selector = jnp.any(
        target[None, :, :] == jnp.arange(experts * capacity)[:, None, None], axis=2
    ).astype(jnp.bfloat16)
    outgoing = (
        jnp.dot(selector, moe_in, preferred_element_type=jnp.float32)
        .astype(jnp.bfloat16)
        .reshape(experts, capacity, model_width)
    )
    gate_matrix = w_gate[0]
    up_matrix = w_up[0]
    down_matrix = w_down[0]
    arrived = lax.all_to_all(outgoing, "grp", split_axis=0, concat_axis=0, tiled=True)
    flattened_rows = arrived.reshape(-1, model_width)
    gate_part = jnp.dot(flattened_rows, gate_matrix, preferred_element_type=jnp.float32)
    up_part = jnp.dot(flattened_rows, up_matrix, preferred_element_type=jnp.float32)
    expert_hidden = (jax.nn.silu(gate_part) * up_part).astype(jnp.bfloat16)
    result = (
        jnp.dot(expert_hidden, down_matrix, preferred_element_type=jnp.float32)
        .astype(jnp.bfloat16)
        .reshape(arrived.shape)
    )
    returned = lax.all_to_all(result, "grp", split_axis=0, concat_axis=0, tiled=True)
    back_rows = returned.reshape(experts * capacity, model_width)
    slots = jnp.arange(experts * capacity)[None, :]
    first_pick = (target[:, 0:1] == slots).astype(half)
    second_pick = (target[:, 1:2] == slots).astype(half)
    first_out = jnp.dot(first_pick, back_rows, preferred_element_type=jnp.float32)
    second = jnp.dot(second_pick, back_rows, preferred_element_type=jnp.float32)
    pair_weights = route_weights[0]
    layer_out = mixed_float + pair_weights[:, 0:1] * first_out + pair_weights[:, 1:2] * second
    return layer_out.astype(jnp.bfloat16)[None]


def solution(mesh):
    in_specs = (
        P("grp", "seq", None),
        P(),
        P("grp", "seq", None),
        P(),
        P(),
        P("grp", "seq", None),
        P(),
        P("grp", None),
        P("grp", "seq", None),
        P(),
        P("grp", None, None),
        P("grp", None, None),
        P("grp", None, None),
        P("grp", "seq", None),
        P("grp", "seq", None),
    )
    out_specs = P("grp", "seq", None)
    return jax.shard_map(
        on_device, mesh=mesh, in_specs=in_specs, out_specs=out_specs, check_vma=False
    )
```

profile of v0, /device:TPU:0, one launch (start us, length us, event | category | flops | bytes accessed | tf_op | source)
XLA Modules:
  0.0 336.8 jit_solution(5236764994432943655)
XLA Ops:
  6.5 1.5 slice_bitcast_fusion
  8.1 2.9 collective-permute-start
  15.1 5.7 %all-gather = f32[4,1,40]{2,1,0:T(1,128)S(1)} all-gather(f32[1,1,40]{2,1,0:T(1,128)S(1)} %get-tuple-element.13), channel_id=1, replica_groups=mesh['seq'=4,'grp'=8] {'seq'}, dimensions={0}, use_global_device_ids=true | all-gather | bytes 800 | tf_op jit(solution)/shard_map/all_gather | solution.py:79
  21.3 1.4 copy.70
  22.8 1.5 copy.75
  25.1 2.4 copy.79
  27.5 1.9 copy.71
  29.5 1.6 maximum_convert_fusion
  31.1 2.9 multiply_convert_fusion.1
  34.4 2.2 collective-permute-start.1
  36.6 3.3 collective-permute-start.2
  39.9 1.3 collective-permute-start.3
  41.5 1.1 convolution_bitcast_fusion
  42.6 12.4 %collective-permute-done.2 = bf16[40,64,64]{2,1,0:T(8,128)(2,1)S(1)} collective-permute-done((bf16[40,64,64]{2,1,0:T(8,128)(2,1)S(1)}, bf16[40,64,64]{2,1,0:T(8,128)(2,1)S(1)}, u32[]{:S(2)}, u32[]{:S(2)}) %collective-permute-start.2) | collective-permute-done | bytes 327712 | tf_op jit(solution)/shard_map/ppermute | solution.py:12
  55.0 11.2 %collective-permute-done.3 = bf16[40,64,64]{2,1,0:T(8,128)(2,1)S(1)} collective-permute-done((bf16[40,64,64]{2,1,0:T(8,128)(2,1)S(1)}, bf16[40,64,64]{2,1,0:T(8,128)(2,1)S(1)}, u32[]{:S(2)}, u32[]{:S(2)}) %collective-permute-start.3) | collective-permute-done | bytes 327712 | tf_op jit(solution)/shard_map/ppermute | solution.py:12
  66.3 2.0 multiply_reduce_fusion
  68.3 2.9 copy.78
  71.1 2.6 fusion.33
  73.8 1.8 constant_dynamic-slice_fusion
  76.5 24.7 %all-gather.4.cloned.1.call-done = bf16[512,2560]{1,0:T(8,128)(2,1)} async-done(((bf16[128,2560]{1,0:T(8,128)(2,1)}), bf16[512,2560]{1,0:T(8,128)(2,1)}) %all-gather.4.cloned.1.call-update) | async-done | bytes 2621456 | tf_op jit(solution)/shard_map/all_gather | solution.py:99
  101.2 64.2 %all-gather.6.cloned.1.call-done = bf16[2560,640]{1,0:T(8,128)(2,1)} async-done(((bf16[320,640]{1,0:T(8,128)(2,1)}), bf16[2560,640]{1,0:T(8,128)(2,1)}) %all-gather.6.cloned.1.call-update) | async-done | bytes 3276816 | tf_op jit(solution)/shard_map/all_gather | solution.py:36
  165.4 5.7 %convolution_convert_fusion.2 = bf16[512,640]{1,0:T(8,128)(2,1)} fusion(bf16[512,2560]{1,0:T(8,128)(2,1)} %all-gather.4.cloned.1.call-done, bf16[2560,640]{1,0:T(8,128)(2,1)} %all-gather.6.cloned.1.call-done), kind=kOutput, calls=%fused_computation.32 | convolution fusion | flops 1678049280 | bytes 6553600 | tf_op jit(solution)/shard_map/dot_general | solution.py:100
  171.2 3.5 %all-to-all-start = ((bf16[4,128,640]{2,1,0:T(8,128)(2,1)}), bf16[4,128,640]{2,1,0:T(8,128)(2,1)S(1)}, u32[]{:S(2)}, u32[]{:S(2)}) async-start(bf16[4,128,640]{2,1,0:T(8,128)(2,1)} %bitcast.134), calls=%async_computation | async-start | bytes 1310720 | tf_op jit(solution)/shard_map/all_to_all | solution.py:101
  175.5 9.4 %all-to-all-done = bf16[4,128,640]{2,1,0:T(8,128)(2,1)S(1)} async-done(((bf16[4,128,640]{2,1,0:T(8,128)(2,1)}), bf16[4,128,640]{2,1,0:T(8,128)(2,1)S(1)}, u32[]{:S(2)}, u32[]{:S(2)}) %all-to-all-start) | async-done | bytes 655392 | tf_op jit(solution)/shard_map/all_to_all | solution.py:101
  187.3 62.7 %all_to_all.23 = bf16[8,64,2560]{2,1,0:T(8,128)(2,1)S(1)} all-to-all(bf16[8,64,2560]{2,1,0:T(8,128)(2,1)S(1)} %bitcast.123), channel_id=1, replica_groups=mesh['seq'=4,'grp'=8] {'grp'}, dimensions={0} | all-to-all | bytes 5242880 | tf_op jit(solution)/shard_map/all_to_all | solution.py:128
  250.0 1.5 copy-done.1
  251.5 2.5 fusion.7
  254.1 7.2 %convolution_convert_fusion = bf16[512,2560]{1,0:T(8,128)(2,1)} fusion(bf16[1,512,2560]{2,1,0:T(8,128)(2,1)S(1)} %copy-done, bf16[512,2560]{1,0:T(8,128)(2,1)} %bitcast.128, bf16[1,2560,512]{2,1,0:T(8,128)(2,1)} %param.26, f32[512,512]{1,0:T(8,128)} %fusion.7), kind=kOutput, calls=%fused_computation | convolution fusion | flops 2687238144 | bytes 11534336 | tf_op jit(solution)/shard_map/dot_general | solution.py:134
  261.3 4.5 %all-to-all-start.2 = ((bf16[8,64,2560]{2,1,0:T(8,128)(2,1)}), bf16[8,64,2560]{2,1,0:T(8,128)(2,1)}, u32[]{:S(2)}, u32[]{:S(2)}) async-start(bf16[8,64,2560]{2,1,0:T(8,128)(2,1)} %bitcast.126), calls=%async_computation.2 | async-start | bytes 5242880 | tf_op jit(solution)/shard_map/all_to_all | solution.py:138
  266.2 58.2 %all-to-all-done.2 = bf16[8,64,2560]{2,1,0:T(8,128)(2,1)} async-done(((bf16[8,64,2560]{2,1,0:T(8,128)(2,1)}), bf16[8,64,2560]{2,1,0:T(8,128)(2,1)}, u32[]{:S(2)}, u32[]{:S(2)}) %all-to-all-start.2) | async-done | bytes 2621472 | tf_op jit(solution)/shard_map/all_to_all | solution.py:138
  324.4 2.3 convolution_multiply_fusion
  326.7 3.2 fusion.3
  (75 shorter events, 10.4 us)
Async XLA Ops:
  6.5 247.5 %copy-start = (bf16[1,512,2560]{2,1,0:T(8,128)(2,1)S(1)}, bf16[1,512,2560]{2,1,0:T(8,128)(2,1)}, u32[]{:S(2)}) copy-start(bf16[1,512,2560]{2,1,0:T(8,128)(2,1)} %param.27) | copy-start | bytes 7864324
  6.5 94.7 %all-gather.4.cloned.1.call-start = ((), (), s32[]{:S(2)}) async-start(), calls=%async_computation.3 | async-start | bytes 3276800 | tf_op jit(solution)/shard_map/all_gather | solution.py:99
  8.1 19.4 %collective-permute-start = (bf16[3,2688]{1,0:T(4,128)(2,1)}, bf16[3,2688]{1,0:T(4,128)(2,1)}, u32[]{:S(2)}, u32[]{:S(2)}) collective-permute-start(bf16[3,2688]{1,0:T(4,128)(2,1)} %slice_bitcast_fusion), channel_id=1, source_target_pairs={{0,8},{8,16},{16,24},{1,9},{9,17},{17,25},{2,10},{10,18},{18,26},{... | collective-permute-start | bytes 48392 | tf_op jit(solution)/shard_map/ppermute | solution.py:12
  34.0 7.4 %copy-start.5 = (f32[40,128]{1,0:T(8,128)S(1)}, f32[40,128]{1,0:T(8,128)}, u32[]{:S(2)}) copy-start(f32[40,128]{1,0:T(8,128)} %copy.75) | copy-start | bytes 61444
  34.0 7.4 %copy-start.6 = (f32[40,128]{1,0:T(8,128)S(1)}, f32[40,128]{1,0:T(8,128)}, u32[]{:S(2)}) copy-start(f32[40,128]{1,0:T(8,128)} %copy.73) | copy-start | bytes 61444
  34.0 7.4 %copy-start.7 = (pred[128,128]{1,0:T(8,128)(4,1)S(1)}, pred[128,128]{1,0:T(8,128)(4,1)}, u32[]{:S(2)}) copy-start(pred[128,128]{1,0:T(8,128)(4,1)} %iota_compare_fusion.5) | copy-start | bytes 49156
  34.4 8.2 %collective-permute-start.1 = (bf16[40,64,64]{2,1,0:T(8,128)(2,1)S(1)}, bf16[40,64,64]{2,1,0:T(8,128)(2,1)S(1)}, u32[]{:S(2)}, u32[]{:S(2)}) collective-permute-start(bf16[40,64,64]{2,1,0:T(8,128)(2,1)S(1)} %convolution_convert_fusion.3), channel_id=1, source_target_pairs={{0,8},{8,16},{16,24},{1,9},{9,17},{17,25},{2,10},{10,18},{18,26},{... | collective-permute-start | bytes 983048 | tf_op jit(solution)/shard_map/ppermute | solution.py:12
  36.6 18.5 %collective-permute-start.2 = (bf16[40,64,64]{2,1,0:T(8,128)(2,1)S(1)}, bf16[40,64,64]{2,1,0:T(8,128)(2,1)S(1)}, u32[]{:S(2)}, u32[]{:S(2)}) collective-permute-start(bf16[40,64,64]{2,1,0:T(8,128)(2,1)S(1)} %convolution_convert_fusion.3), channel_id=1, source_target_pairs={{0,16},{8,24},{1,17},{9,25},{2,18},{10,26},{3,19},{11,27},{4,20},{... | collective-permute-start | bytes 983048 | tf_op jit(solution)/shard_map/ppermute | solution.py:12
  39.9 26.3 %collective-permute-start.3 = (bf16[40,64,64]{2,1,0:T(8,128)(2,1)S(1)}, bf16[40,64,64]{2,1,0:T(8,128)(2,1)S(1)}, u32[]{:S(2)}, u32[]{:S(2)}) collective-permute-start(bf16[40,64,64]{2,1,0:T(8,128)(2,1)S(1)} %convolution_convert_fusion.3), channel_id=1, source_target_pairs={{0,24},{1,25},{2,26},{3,27},{4,28},{5,29},{6,30},{7,31}} | collective-permute-start | bytes 983048 | tf_op jit(solution)/shard_map/ppermute | solution.py:12
  41.5 24.8 %copy-start.3 = (f32[1,128,2560]{1,2,0:T(8,128)S(1)}, f32[1,128,2560]{1,2,0:T(8,128)}, u32[]{:S(2)}) copy-start(f32[1,128,2560]{1,2,0:T(8,128)} %copy.79) | copy-start | bytes 3932164
  41.5 24.8 %copy-start.12 = (f32[40]{0:T(128)S(1)}, f32[40]{0:T(128)}, u32[]{:S(2)}) copy-start(f32[40]{0:T(128)} %get-tuple-element.18) | copy-start | bytes 484
  41.5 24.8 %copy-start.13 = (f32[40]{0:T(128)S(1)}, f32[40]{0:T(128)}, u32[]{:S(2)}) copy-start(f32[40]{0:T(128)} %get-tuple-element.19) | copy-start | bytes 484
  41.5 24.7 %copy-start.15 = (f32[40]{0:T(128)S(1)}, f32[40]{0:T(128)}, u32[]{:S(2)}) copy-start(f32[40]{0:T(128)} %param.19) | copy-start | bytes 484
  68.3 2.9 copy-start.2
  68.3 2.9 copy-start.8
  73.8 1.9 copy-start.10
  73.8 91.6 %all-gather.6.cloned.1.call-start = ((), (), s32[]{:S(2)}) async-start(), calls=%async_computation.4 | async-start | bytes 3686400 | tf_op jit(solution)/shard_map/all_gather | solution.py:36
  171.2 13.7 %all-to-all-start = ((bf16[4,128,640]{2,1,0:T(8,128)(2,1)}), bf16[4,128,640]{2,1,0:T(8,128)(2,1)S(1)}, u32[]{:S(2)}, u32[]{:S(2)}) async-start(bf16[4,128,640]{2,1,0:T(8,128)(2,1)} %bitcast.134), calls=%async_computation | async-start | bytes 1310720 | tf_op jit(solution)/shard_map/all_to_all | solution.py:101
  185.0 1.1 copy-start.4
  185.1 1.2 copy-start.9
  187.3 64.2 %copy-start.14 = (bf16[1,2560,512]{2,1,0:T(8,128)(2,1)S(1)}, bf16[1,2560,512]{2,1,0:T(8,128)(2,1)}, u32[]{:S(2)}) copy-start(bf16[1,2560,512]{2,1,0:T(8,128)(2,1)} %param.25) | copy-start | bytes 7864324
  250.0 1.5 copy-start.1
  261.3 4.9 %copy-start.11 = (f32[1,128,2]{1,2,0:T(2,128)S(1)}, f32[1,128,2]{1,2,0:T(2,128)}, u32[]{:S(2)}) copy-start(f32[1,128,2]{1,2,0:T(2,128)} %param.29) | copy-start | bytes 3076
  261.3 63.1 %all-to-all-start.2 = ((bf16[8,64,2560]{2,1,0:T(8,128)(2,1)}), bf16[8,64,2560]{2,1,0:T(8,128)(2,1)}, u32[]{:S(2)}, u32[]{:S(2)}) async-start(bf16[8,64,2560]{2,1,0:T(8,128)(2,1)} %bitcast.126), calls=%async_computation.2 | async-start | bytes 5242880 | tf_op jit(solution)/shard_map/all_to_all | solution.py:138
Sparse Core Ops, SparseCore 0:
  73.9 27.2 all-gather.3
  103.4 61.9 all-gather.5
where the time goes:
time: 338 us; the launch traced here: 337 us
  waiting for transfers between devices  180 us (53%)
  blocking collectives  68.3 us (20%)
  matrix products  25.6 us (8%)
  local copies, waits for them, and re-layouts  20.7 us (6%)
  starting transfers between devices  17.8 us (5%)
  between operations  13.7 us (4%)
  other arithmetic  10.4 us (3%)
    all_gather x1, waiting for transfers between devices, on_device(): lax.all_gather(lax.dynamic_slice_in_dim(out_weight, own * share, share, a...  64.2 us
    all_to_all x1, blocking collectives, on_device(): lax.all_to_all(outgoing, 'grp', split_axis=0, concat_axis=0, tiled=True)  62.7 us
    all_to_all x1, waiting for transfers between devices, on_device(): lax.all_to_all(result, 'grp', split_axis=0, concat_axis=0, tiled=True)  58.2 us
    all_gather x1, waiting for transfers between devices, on_device(): all_rows = lax.all_gather(normed, 'seq', axis=0, tiled=True)  24.7 us
    ppermute x4, waiting for transfers between devices, from_behind(): lax.ppermute(value, axis, [(source, source + steps) for source in range(f...  23.6 us
    ppermute x4, starting transfers between devices, from_behind(): lax.ppermute(value, axis, [(source, source + steps) for source in range(f...  9.76 us
    all_to_all x1, waiting for transfers between devices, on_device(): lax.all_to_all(column_share, 'seq', split_axis=0, concat_axis=1, tiled=True)  9.41 us
    dot_general x1, matrix products, on_device(): jnp.dot(expert_hidden, down_matrix, preferred_element_type=jnp.float32)  7.24 us
  transfers between devices with their start and end apart: 8, of which 6 were waited for; matrix products, arithmetic and copies ran while one was open for 5% of the time, Pallas kernels for 0%

commit v1 on v0

--- a/solution.py
+++ b/solution.py
@@ -96,7 +96,14 @@
     normed = (gated_out * lax.rsqrt(mean_square + EPSILON) * norm_gain[None, :]).astype(
         jnp.bfloat16
     )
-    all_rows = lax.all_gather(normed, "seq", axis=0, tiled=True)
+    ring_ = [normed]
+    for hop in range(3):
+        ring_.append(lax.ppermute(ring_[-1], "seq", [(dev, (dev + 1) % 4) for dev in range(4)]))
+    all_rows = jnp.roll(
+        jnp.concatenate(ring_[::-1], axis=0),
+        (lax.axis_index("seq") + 1) * ring_[0].shape[0],
+        axis=0,
+    )
     column_share = jnp.dot(all_rows, weight_share, preferred_element_type=jnp.float32).astype(half)
     projected = lax.all_to_all(column_share, "seq", split_axis=0, concat_axis=1, tiled=True).astype(
         jnp.float32

time: 338 us -> 292 us (0.86)
  waiting for transfers between devices: 180 us -> 121 us
  local copies, waits for them, and re-layouts: 20.7 us -> 31.6 us
    all_gather x1, waiting for transfers between devices: 64.2 us -> 0.01 us  [on_device(): lax.all_gather(lax.dynamic_slice_in_dim(out_weight, own * share, share, a...]
    ppermute x0 -> x3, waiting for transfers between devices: none -> 29.8 us  [on_device(): lax.ppermute(ring_[-1], 'seq', [(dev, (dev + 1) % 4) for dev in range(4)])]
    all_gather x1 -> x0, waiting for transfers between devices: 24.7 us -> none  [on_device(): all_rows = lax.all_gather(normed, 'seq', axis=0, tiled=True)]
    unnamed x36 -> x49, local copies, waits for them, and re-layouts: 4.92 us -> 15.6 us
  transfers between devices with their start and end apart: 8 -> 10, of which waited for: 6 -> 7; matrix products, arithmetic and copies ran while one was open for 5% -> 14% of each run, Pallas kernels for 0% -> 0%
where the time goes in v1:
time: 292 us; the launch traced here: 291 us
  waiting for transfers between devices  121 us (41%)
  blocking collectives  71.4 us (24%)
  local copies, waits for them, and re-layouts  31.6 us (11%)
  matrix products  25.6 us (9%)
  starting transfers between devices  17.8 us (6%)
  between operations  13.8 us (5%)
  other arithmetic  9.74 us (3%)
    all_to_all x1, blocking collectives, on_device(): lax.all_to_all(outgoing, 'grp', split_axis=0, concat_axis=0, tiled=True)  65.7 us
    all_to_all x1, waiting for transfers between devices, on_device(): lax.all_to_all(result, 'grp', split_axis=0, concat_axis=0, tiled=True)  58.2 us
    ppermute x3, waiting for transfers between devices, on_device(): lax.ppermute(ring_[-1], 'seq', [(dev, (dev + 1) % 4) for dev in range(4)])  29.8 us
    ppermute x4, waiting for transfers between devices, from_behind(): lax.ppermute(value, axis, [(source, source + steps) for source in range(f...  23.6 us
    unnamed x49, local copies, waits for them, and re-layouts  15.6 us
    ppermute x4, starting transfers between devices, from_behind(): lax.ppermute(value, axis, [(source, source + steps) for source in range(f...  9.75 us
    all_to_all x1, waiting for transfers between devices, on_device(): lax.all_to_all(column_share, 'seq', split_axis=0, concat_axis=1, tiled=True)  9.41 us
    dot_general x1, matrix products, on_device(): jnp.dot(expert_hidden, down_matrix, preferred_element_type=jnp.float32)  7.24 us
  transfers between devices with their start and end apart: 10, of which 7 were waited for; matrix products, arithmetic and copies ran while one was open for 14% of the time, Pallas kernels for 0%

profile of v1, /device:TPU:0, one launch (start us, length us, event | category | flops | bytes accessed | tf_op | source)
XLA Modules:
  0.0 291.0 jit_solution(4322513391719245790)
XLA Ops:
  6.5 1.5 slice_bitcast_fusion
  8.1 2.9 %collective-permute-start = (bf16[3,2688]{1,0:T(4,128)(2,1)}, bf16[3,2688]{1,0:T(4,128)(2,1)}, u32[]{:S(2)}, u32[]{:S(2)}) collective-permute-start(bf16[3,2688]{1,0:T(4,128)(2,1)} %slice_bitcast_fusion), channel_id=1, source_target_pairs={{0,8},{8,16},{16,24},{1,9},{9,17},{17,25},{2,10},{10,18},{18,26},{... | collective-permute-start | bytes 48392 | tf_op jit(solution)/shard_map/ppermute | solution.py:12
  11.0 1.8 constant_dynamic-slice_fusion
  15.6 5.7 %all-gather = f32[4,1,40]{2,1,0:T(1,128)S(1)} all-gather(f32[1,1,40]{2,1,0:T(1,128)S(1)} %get-tuple-element.13), channel_id=1, replica_groups=mesh['seq'=4,'grp'=8] {'seq'}, dimensions={0}, use_global_device_ids=true | all-gather | bytes 800 | tf_op jit(solution)/shard_map/all_gather | solution.py:79
  25.7 2.4 copy.79
  28.1 1.9 copy.71
  30.0 1.6 maximum_convert_fusion
  31.6 2.9 multiply_convert_fusion.1
  35.0 2.1 collective-permute-start.1
  37.1 3.3 %collective-permute-start.2 = (bf16[40,64,64]{2,1,0:T(8,128)(2,1)S(1)}, bf16[40,64,64]{2,1,0:T(8,128)(2,1)S(1)}, u32[]{:S(2)}, u32[]{:S(2)}) collective-permute-start(bf16[40,64,64]{2,1,0:T(8,128)(2,1)S(1)} %convolution_convert_fusion.2), channel_id=1, source_target_pairs={{0,16},{8,24},{1,17},{9,25},{2,18},{10,26},{3,19},{11,27},{4,20},{... | collective-permute-start | bytes 983048 | tf_op jit(solution)/shard_map/ppermute | solution.py:12
  43.2 12.4 %collective-permute-done.2 = bf16[40,64,64]{2,1,0:T(8,128)(2,1)S(1)} collective-permute-done((bf16[40,64,64]{2,1,0:T(8,128)(2,1)S(1)}, bf16[40,64,64]{2,1,0:T(8,128)(2,1)S(1)}, u32[]{:S(2)}, u32[]{:S(2)}) %collective-permute-start.2) | collective-permute-done | bytes 327712 | tf_op jit(solution)/shard_map/ppermute | solution.py:12
  55.6 11.2 %collective-permute-done.3 = bf16[40,64,64]{2,1,0:T(8,128)(2,1)S(1)} collective-permute-done((bf16[40,64,64]{2,1,0:T(8,128)(2,1)S(1)}, bf16[40,64,64]{2,1,0:T(8,128)(2,1)S(1)}, u32[]{:S(2)}, u32[]{:S(2)}) %collective-permute-start.3) | collective-permute-done | bytes 327712 | tf_op jit(solution)/shard_map/ppermute | solution.py:12
  66.8 2.0 multiply_reduce_fusion
  68.8 2.8 copy.78
  71.6 1.9 fusion.38
  73.6 10.2 %collective-permute-done.4 = bf16[128,2560]{1,0:T(8,128)(2,1)S(1)} collective-permute-done((bf16[128,2560]{1,0:T(8,128)(2,1)S(1)}, bf16[128,2560]{1,0:T(8,128)(2,1)S(1)}, u32[]{:S(2)}, u32[]{:S(2)}) %collective-permute-start.4) | collective-permute-done | bytes 655392 | tf_op jit(solution)/shard_map/ppermute | solution.py:101
  84.7 10.1 %collective-permute-done.5 = bf16[128,2560]{1,0:T(8,128)(2,1)} collective-permute-done((bf16[128,2560]{1,0:T(8,128)(2,1)S(1)}, bf16[128,2560]{1,0:T(8,128)(2,1)}, u32[]{:S(2)}, u32[]{:S(2)}) %collective-permute-start.5) | collective-permute-done | bytes 655392 | tf_op jit(solution)/shard_map/ppermute | solution.py:101
  95.6 9.5 %collective-permute-done.6 = bf16[128,2560]{1,0:T(8,128)(2,1)} collective-permute-done((bf16[128,2560]{1,0:T(8,128)(2,1)}, bf16[128,2560]{1,0:T(8,128)(2,1)}, u32[]{:S(2)}, u32[]{:S(2)}) %collective-permute-start.6) | collective-permute-done | bytes 655392 | tf_op jit(solution)/shard_map/ppermute | solution.py:101
  105.1 2.0 constant_dynamic-update-slice_fusion.7
  107.1 2.0 constant_dynamic-update-slice_fusion.6
  110.8 2.0 constant_dynamic-update-slice_fusion.3
  112.8 2.0 constant_dynamic-update-slice_fusion.2
  116.6 5.7 %fusion.19 = bf16[512,640]{1,0:T(8,128)(2,1)} fusion(bf16[2560,640]{1,0:T(8,128)(2,1)} %all-gather.3.cloned.1.call-done, bf16[1024,2560]{1,0:T(8,128)(2,1)} %constant_dynamic-update-slice_fusion, s32[]{:T(128)S(6)} %select_n.37), kind=kOutput, calls=%fused_computation.34 | convolution fusion | flops 1678049280 | bytes 6553604 | tf_op jit(solution)/shard_map/dot_general | solution.py:107
  122.3 3.5 %all-to-all-start = ((bf16[4,128,640]{2,1,0:T(8,128)(2,1)}), bf16[4,128,640]{2,1,0:T(8,128)(2,1)S(1)}, u32[]{:S(2)}, u32[]{:S(2)}) async-start(bf16[4,128,640]{2,1,0:T(8,128)(2,1)} %bitcast.133), calls=%async_computation | async-start | bytes 1310720 | tf_op jit(solution)/shard_map/all_to_all | solution.py:108
  126.6 9.4 %all-to-all-done = bf16[4,128,640]{2,1,0:T(8,128)(2,1)S(1)} async-done(((bf16[4,128,640]{2,1,0:T(8,128)(2,1)}), bf16[4,128,640]{2,1,0:T(8,128)(2,1)S(1)}, u32[]{:S(2)}, u32[]{:S(2)}) %all-to-all-start) | async-done | bytes 655392 | tf_op jit(solution)/shard_map/all_to_all | solution.py:108
  138.5 65.7 %all_to_all.23 = bf16[8,64,2560]{2,1,0:T(8,128)(2,1)S(1)} all-to-all(bf16[8,64,2560]{2,1,0:T(8,128)(2,1)S(1)} %bitcast.122), channel_id=1, replica_groups=mesh['seq'=4,'grp'=8] {'grp'}, dimensions={0} | all-to-all | bytes 5242880 | tf_op jit(solution)/shard_map/all_to_all | solution.py:135
  205.7 2.5 fusion.7
  208.3 7.2 %convolution_convert_fusion = bf16[512,2560]{1,0:T(8,128)(2,1)} fusion(bf16[1,512,2560]{2,1,0:T(8,128)(2,1)S(1)} %copy-done, bf16[512,2560]{1,0:T(8,128)(2,1)} %bitcast.127, bf16[1,2560,512]{2,1,0:T(8,128)(2,1)} %param.26, f32[512,512]{1,0:T(8,128)} %fusion.7), kind=kOutput, calls=%fused_computation | convolution fusion | flops 2687238144 | bytes 11534336 | tf_op jit(solution)/shard_map/dot_general | solution.py:141
  215.5 4.5 %all-to-all-start.2 = ((bf16[8,64,2560]{2,1,0:T(8,128)(2,1)}), bf16[8,64,2560]{2,1,0:T(8,128)(2,1)}, u32[]{:S(2)}, u32[]{:S(2)}) async-start(bf16[8,64,2560]{2,1,0:T(8,128)(2,1)} %bitcast.125), calls=%async_computation.2 | async-start | bytes 5242880 | tf_op jit(solution)/shard_map/all_to_all | solution.py:145
  220.4 58.2 %all-to-all-done.2 = bf16[8,64,2560]{2,1,0:T(8,128)(2,1)} async-done(((bf16[8,64,2560]{2,1,0:T(8,128)(2,1)}), bf16[8,64,2560]{2,1,0:T(8,128)(2,1)}, u32[]{:S(2)}, u32[]{:S(2)}) %all-to-all-start.2) | async-done | bytes 2621472 | tf_op jit(solution)/shard_map/all_to_all | solution.py:145
  278.6 2.3 convolution_multiply_fusion
  280.9 3.2 %fusion.3 = bf16[1,128,2560]{2,1,0:T(8,128)(2,1)} fusion(f32[128,2560]{1,0:T(8,128)S(1)} %convolution_multiply_fusion, bf16[512,2560]{1,0:T(8,128)(2,1)} %bitcast.31, bf16[128,2560]{1,0:T(8,128)(2,1)S(1)} %get-tuple-element.12, f32[128]{0:T(128)S(1)} %get-tuple-element.20, s32[128]{0:T(128)S(1)} %get-tuple-element.5), kind=kOutput, calls=%fused_computation.7 | convolution fusion | flops 337248256 | bytes 5243904 | tf_op jit(solution)/shard_map/dot_general | solution.py:150
  (92 shorter events, 20.4 us)
Async XLA Ops:
  6.5 201.7 %copy-start = (bf16[1,512,2560]{2,1,0:T(8,128)(2,1)S(1)}, bf16[1,512,2560]{2,1,0:T(8,128)(2,1)}, u32[]{:S(2)}) copy-start(bf16[1,512,2560]{2,1,0:T(8,128)(2,1)} %param.27) | copy-start | bytes 7864324
  6.5 8.0 %copy-start.6 = (f32[1,128,40]{1,2,0:T(8,128)S(1)}, f32[1,128,40]{1,2,0:T(8,128)}, u32[]{:S(2)}) copy-start(f32[1,128,40]{1,2,0:T(8,128)} %param.17) | copy-start | bytes 61444
  6.5 8.1 %copy-start.17 = (f32[40]{0:T(128)S(1)}, f32[40]{0:T(128)}, u32[]{:S(2)}) copy-start(f32[40]{0:T(128)} %param.18) | copy-start | bytes 484
  6.5 110.0 %all-gather.3.cloned.1.call-start = ((), (), s32[]{:S(2)}) async-start(), calls=%async_computation.3 | async-start | bytes 3686400 | tf_op jit(solution)/shard_map/all_gather | solution.py:36
  8.1 20.0 %collective-permute-start = (bf16[3,2688]{1,0:T(4,128)(2,1)}, bf16[3,2688]{1,0:T(4,128)(2,1)}, u32[]{:S(2)}, u32[]{:S(2)}) collective-permute-start(bf16[3,2688]{1,0:T(4,128)(2,1)} %slice_bitcast_fusion), channel_id=1, source_target_pairs={{0,8},{8,16},{16,24},{1,9},{9,17},{17,25},{2,10},{10,18},{18,26},{... | collective-permute-start | bytes 48392 | tf_op jit(solution)/shard_map/ppermute | solution.py:12
  34.5 7.4 %copy-start.7 = (f32[40,128]{1,0:T(8,128)S(1)}, f32[40,128]{1,0:T(8,128)}, u32[]{:S(2)}) copy-start(f32[40,128]{1,0:T(8,128)} %copy.75) | copy-start | bytes 61444
  34.6 7.4 %copy-start.8 = (f32[40,128]{1,0:T(8,128)S(1)}, f32[40,128]{1,0:T(8,128)}, u32[]{:S(2)}) copy-start(f32[40,128]{1,0:T(8,128)} %copy.73) | copy-start | bytes 61444
  34.6 7.4 %copy-start.9 = (pred[128,128]{1,0:T(8,128)(4,1)S(1)}, pred[128,128]{1,0:T(8,128)(4,1)}, u32[]{:S(2)}) copy-start(pred[128,128]{1,0:T(8,128)(4,1)} %iota_compare_fusion.5) | copy-start | bytes 49156
  35.0 8.2 %collective-permute-start.1 = (bf16[40,64,64]{2,1,0:T(8,128)(2,1)S(1)}, bf16[40,64,64]{2,1,0:T(8,128)(2,1)S(1)}, u32[]{:S(2)}, u32[]{:S(2)}) collective-permute-start(bf16[40,64,64]{2,1,0:T(8,128)(2,1)S(1)} %convolution_convert_fusion.2), channel_id=1, source_target_pairs={{0,8},{8,16},{16,24},{1,9},{9,17},{17,25},{2,10},{10,18},{18,26},{... | collective-permute-start | bytes 983048 | tf_op jit(solution)/shard_map/ppermute | solution.py:12
  37.1 18.5 %collective-permute-start.2 = (bf16[40,64,64]{2,1,0:T(8,128)(2,1)S(1)}, bf16[40,64,64]{2,1,0:T(8,128)(2,1)S(1)}, u32[]{:S(2)}, u32[]{:S(2)}) collective-permute-start(bf16[40,64,64]{2,1,0:T(8,128)(2,1)S(1)} %convolution_convert_fusion.2), channel_id=1, source_target_pairs={{0,16},{8,24},{1,17},{9,25},{2,18},{10,26},{3,19},{11,27},{4,20},{... | collective-permute-start | bytes 983048 | tf_op jit(solution)/shard_map/ppermute | solution.py:12
  40.5 26.3 %collective-permute-start.3 = (bf16[40,64,64]{2,1,0:T(8,128)(2,1)S(1)}, bf16[40,64,64]{2,1,0:T(8,128)(2,1)S(1)}, u32[]{:S(2)}, u32[]{:S(2)}) collective-permute-start(bf16[40,64,64]{2,1,0:T(8,128)(2,1)S(1)} %convolution_convert_fusion.2), channel_id=1, source_target_pairs={{0,24},{1,25},{2,26},{3,27},{4,28},{5,29},{6,30},{7,31}} | collective-permute-start | bytes 983048 | tf_op jit(solution)/shard_map/ppermute | solution.py:12
  42.0 24.8 %copy-start.4 = (f32[1,128,2560]{1,2,0:T(8,128)S(1)}, f32[1,128,2560]{1,2,0:T(8,128)}, u32[]{:S(2)}) copy-start(f32[1,128,2560]{1,2,0:T(8,128)} %copy.79) | copy-start | bytes 3932164
  42.0 24.8 %copy-start.14 = (f32[40]{0:T(128)S(1)}, f32[40]{0:T(128)}, u32[]{:S(2)}) copy-start(f32[40]{0:T(128)} %get-tuple-element.18) | copy-start | bytes 484
  42.0 24.8 %copy-start.15 = (f32[40]{0:T(128)S(1)}, f32[40]{0:T(128)}, u32[]{:S(2)}) copy-start(f32[40]{0:T(128)} %get-tuple-element.19) | copy-start | bytes 484
  42.0 24.8 %copy-start.18 = (f32[40]{0:T(128)S(1)}, f32[40]{0:T(128)}, u32[]{:S(2)}) copy-start(f32[40]{0:T(128)} %param.19) | copy-start | bytes 484
  68.8 2.8 copy-start.10
  71.6 23.2 %copy-start.12 = (s32[1,128,2]{1,2,0:T(2,128)S(1)}, s32[1,128,2]{1,2,0:T(2,128)}, u32[]{:S(2)}) copy-start(s32[1,128,2]{1,2,0:T(2,128)} %param.28) | copy-start | bytes 3076
  73.6 10.2 %collective-permute-start.4 = (bf16[128,2560]{1,0:T(8,128)(2,1)S(1)}, bf16[128,2560]{1,0:T(8,128)(2,1)S(1)}, u32[]{:S(2)}, u32[]{:S(2)}) collective-permute-start(bf16[128,2560]{1,0:T(8,128)(2,1)S(1)} %fusion.38), channel_id=1, source_target_pairs={{0,8},{8,16},{16,24},{24,0},{1,9},{9,17},{17,25},{25,1},{2,10},{10... | collective-permute-start | bytes 1966088 | tf_op jit(solution)/shard_map/ppermute | solution.py:101
  83.8 0.8 copy-start.2
  84.7 10.1 %collective-permute-start.5 = (bf16[128,2560]{1,0:T(8,128)(2,1)S(1)}, bf16[128,2560]{1,0:T(8,128)(2,1)}, u32[]{:S(2)}, u32[]{:S(2)}) collective-permute-start(bf16[128,2560]{1,0:T(8,128)(2,1)S(1)} %collective-permute-done.4), channel_id=1, source_target_pairs={{0,8},{8,16},{16,24},{24,0},{1,9},{9,17},{17,25},{25,1},{2,10},{10... | collective-permute-start | bytes 1966088 | tf_op jit(solution)/shard_map/ppermute | solution.py:101
  94.8 10.3 %collective-permute-start.6 = (bf16[128,2560]{1,0:T(8,128)(2,1)}, bf16[128,2560]{1,0:T(8,128)(2,1)}, u32[]{:S(2)}, u32[]{:S(2)}) collective-permute-start(bf16[128,2560]{1,0:T(8,128)(2,1)} %collective-permute-done.5), channel_id=1, source_target_pairs={{0,8},{8,16},{16,24},{24,0},{1,9},{9,17},{17,25},{25,1},{2,10},{10... | collective-permute-start | bytes 1966088 | tf_op jit(solution)/shard_map/ppermute | solution.py:101
  95.6 13.4 %copy-start.3 = (bf16[128,2560]{1,0:T(8,128)(2,1)S(1)}, bf16[128,2560]{1,0:T(8,128)(2,1)}, u32[]{:S(2)}) copy-start(bf16[128,2560]{1,0:T(8,128)(2,1)} %copy-done.2) | copy-start | bytes 1966084
  122.3 13.7 %all-to-all-start = ((bf16[4,128,640]{2,1,0:T(8,128)(2,1)}), bf16[4,128,640]{2,1,0:T(8,128)(2,1)S(1)}, u32[]{:S(2)}, u32[]{:S(2)}) async-start(bf16[4,128,640]{2,1,0:T(8,128)(2,1)} %bitcast.133), calls=%async_computation | async-start | bytes 1310720 | tf_op jit(solution)/shard_map/all_to_all | solution.py:108
  136.1 1.1 copy-start.5
  136.3 1.2 copy-start.11
  138.5 67.3 %copy-start.16 = (bf16[1,2560,512]{2,1,0:T(8,128)(2,1)S(1)}, bf16[1,2560,512]{2,1,0:T(8,128)(2,1)}, u32[]{:S(2)}) copy-start(bf16[1,2560,512]{2,1,0:T(8,128)(2,1)} %param.25) | copy-start | bytes 7864324
  204.2 1.5 copy-start.1
  215.5 4.9 %copy-start.13 = (f32[1,128,2]{1,2,0:T(2,128)S(1)}, f32[1,128,2]{1,2,0:T(2,128)}, u32[]{:S(2)}) copy-start(f32[1,128,2]{1,2,0:T(2,128)} %param.29) | copy-start | bytes 3076
  215.5 63.1 %all-to-all-start.2 = ((bf16[8,64,2560]{2,1,0:T(8,128)(2,1)}), bf16[8,64,2560]{2,1,0:T(8,128)(2,1)}, u32[]{:S(2)}, u32[]{:S(2)}) async-start(bf16[8,64,2560]{2,1,0:T(8,128)(2,1)} %bitcast.125), calls=%async_computation.2 | async-start | bytes 5242880 | tf_op jit(solution)/shard_map/all_to_all | solution.py:145
Sparse Core Ops, SparseCore 0:
  13.0 63.9 all-gather.2
